TPU v7x, 256 devices: a whole 4x4x8 slice. The times are simulated.
256 devices in a mesh: shift: 8 (over y_lo, x), sub: 32 (over y_hi, z, core).
Axes of the slice: x: 4, y: 4 (y_hi: 2, y_lo: 2; y = y_hi * 2 + y_lo), z: 8, core: 2. Of those that a mesh axis runs over, the one named last changes fastest.
Arguments:
- interior_rhs: bfloat16 [32, 1024, 384], P('sub'), may hold values from -6 to 6
- interface_rhs: bfloat16 [2048, 384], replicated, may hold values from -6 to 6
- interior_inverse: bfloat16 [16, 32, 1024, 1024], P('shift', 'sub'), may hold values from -0.1875 to 0.1875
- coupling: bfloat16 [32, 1024, 256], P('sub'), may hold values from -0.1875 to 0.1875
- schur_inverse: bfloat16 [16, 2048, 2048], P('shift', 'sub'), may hold values from -0.125 to 0.125
- weights: float32 [16], P('shift'), may hold values from -1 to 1
- owner_sub: int32 [32], replicated, may hold values from 0 to 31, each once
- index_blocks: int32 [32, 256], replicated, may hold values from 0 to 2047, as said below
Outputs:
- filtered: float32 [1024, 32, 384], P('shift', 'sub')
Inputs may be any that keep to these rules, and one draw needn't show every extreme that they name: `index_blocks`: each row holds 256 distinct interface unknowns; of each aligned block of 2048 // 32 interface unknowns a row holds at most 16, and exactly 16 of some block. `owner_sub`: each position names a different substructure.
All inputs are finite; a program needn't handle non-finite values.
Results may differ from a plain program's by a relative error of at most 0.0053.
Values may be sent and summed in bfloat16 or wider, within the bound.
No kernel may reach another device: no remote copies, remote signals or barrier semaphores. Data moves between devices by JAX's collectives and lax.ppermute only.
A program may use at most 64 MiB of HBM per device.

v0:
```python
import jax
import jax.numpy as jnp
from jax import lax
from jax.sharding import PartitionSpec as P


def on_device(
    interior_rhs,
    interface_rhs,
    interior_inverse,
    coupling,
    schur_inverse,
    weights,
    owner_sub,
    index_blocks,
):
    position = lax.axis_index("sub")
    substructure = lax.dynamic_index_in_dim(owner_sub, position, 0, keepdims=False)
    idx = lax.dynamic_index_in_dim(index_blocks, substructure, 0, keepdims=False)
    rhs_local = interior_rhs[0]
    couple_local = coupling[0]
    accumulated = jnp.zeros(rhs_local.shape, jnp.float32)
    for which in range(interior_inverse.shape[0]):
        inverse = interior_inverse[which, 0]
        schur_local = schur_inverse[which]
        eliminated = jnp.dot(inverse, rhs_local, preferred_element_type=jnp.float32).astype(
            jnp.bfloat16
        )
        coupled = lax.dot_general(
            couple_local, eliminated, (((0,), (0,)), ((), ())), preferred_element_type=jnp.float32
        ).astype(jnp.bfloat16)
        targets = lax.iota(jnp.int32, interface_rhs.shape[0])
        selector = (idx[None, :] == targets[:, None]).astype(jnp.bfloat16)
        summed_all = lax.psum(jnp.dot(selector, coupled, preferred_element_type=jnp.float32), "sub")
        reduced_all = (interface_rhs.astype(jnp.float32) - summed_all).astype(jnp.bfloat16)
        solved = jnp.dot(schur_local, reduced_all, preferred_element_type=jnp.float32)
        interface_sol = solved.astype(jnp.bfloat16)
        piece = lax.all_gather(interface_sol, "sub", axis=0, tiled=True)
        sources = lax.iota(jnp.int32, piece.shape[0])
        pick_selector = (idx[:, None] == sources[None, :]).astype(jnp.bfloat16)
        picked = jnp.dot(pick_selector, piece, preferred_element_type=jnp.float32)
        correction = jnp.dot(
            couple_local, picked.astype(jnp.bfloat16), preferred_element_type=jnp.float32
        ).astype(jnp.bfloat16)
        interior_sol = eliminated.astype(jnp.float32) - jnp.dot(
            inverse, correction, preferred_element_type=jnp.float32
        )
        accumulated = accumulated + weights[which] * interior_sol
    share_rows = accumulated.shape[0] // lax.axis_size("shift")
    whole_sum = lax.psum(accumulated, "shift")
    own_rows = lax.dynamic_slice_in_dim(
        whole_sum, lax.axis_index("shift") * share_rows, share_rows, 0
    )
    return own_rows[:, None, :]


def solution(mesh):
    in_specs = (
        P("sub", None, None),
        P(),
        P("shift", "sub", None, None),
        P("sub", None, None),
        P("shift", "sub", None),
        P("shift"),
        P(),
        P(),
    )
    out_specs = P("shift", "sub", None)
    return jax.shard_map(
        on_device, mesh=mesh, in_specs=in_specs, out_specs=out_specs, check_vma=False
    )
```

profile of v0, /device:TPU:32, one launch (start us, length us, event | category | flops | bytes accessed | tf_op | source)
XLA Modules:
  0.0 565.3 jit_solution(16608008642296047814)
XLA Ops:
  6.5 1.3 dynamic_slice.11
  9.2 3.0 fusion.27
  12.2 1.3 fusion.30
  14.1 0.7 constant_dynamic-slice_fusion.1
  14.8 3.1 fusion.11
  17.9 3.1 fusion.10
  21.0 0.0 all-reduce.6.cloned.1.call-update
  21.0 0.0 all-gather.5.cloned.1.call-start
  21.1 283.2 %all-reduce.6.cloned.1.call-done = (f32[2048,384]{1,0:T(8,128)}, f32[2048,384]{1,0:T(8,128)}) async-done(((f32[2048,384]{1,0:T(8,128)}, f32[2048,384]{1,0:T(8,128)}), (f32[2048,384]{1,0:T(8,128)}, f32[2048,384]{1,0:T(8,128)})) %all-reduce.6.cloned.1.call-update) | async-done | bytes 6291472 | tf_op jit(solution)/shard_map/psum | solution.py:34
  304.3 3.0 fusion.41
  307.3 0.0 all-gather.5.cloned.1.call-update
  307.4 0.0 all-gather.3.cloned.1.call-start
  307.4 3.0 fusion.44
  310.5 0.0 all-reduce.4.cloned.1.call-start
  310.5 0.6 fusion.65
  311.1 78.0 %all-gather.5.cloned.1.call-done = bf16[2048,384]{1,0:T(8,128)(2,1)} async-done(((bf16[64,384]{1,0:T(8,128)(2,1)}), bf16[2048,384]{1,0:T(8,128)(2,1)}) %all-gather.5.cloned.1.call-update) | async-done | bytes 1572880 | tf_op jit(solution)/shard_map/all_gather | solution.py:38
  389.1 2.2 fusion.34
  391.3 4.2 fusion.2
  395.5 71.4 %all-gather.3.cloned.1.call-done = bf16[2048,384]{1,0:T(8,128)(2,1)} async-done(((bf16[64,384]{1,0:T(8,128)(2,1)}), bf16[2048,384]{1,0:T(8,128)(2,1)}) %all-gather.3.cloned.1.call-update) | async-done | bytes 1572880 | tf_op jit(solution)/shard_map/all_gather | solution.py:38
  466.9 2.2 fusion.33
  469.1 6.1 %fusion.23 = f32[1024,384]{1,0:T(8,128)} fusion(f32[384,1024]{0,1:T(8,128)} %fusion.2, bf16[1024,384]{1,0:T(8,128)(2,1)S(1)} %copy-done.6, bf16[1024,384]{1,0:T(8,128)(2,1)S(1)} %copy-done.4, bf16[2,1,1024,1024]{3,2,1,0:T(8,128)(2,1)} %param.10, bf16[256,384]{1,0:T(8,128)(2,1)S(1)} %fusion.33, f32[]{:T(128)} %bitcast.9, f32[]{:T(128)} %bitcast, ...), kind=kOutput, calls=%fused_computation.26 | convolution fusion | flops 1009778688 | bytes 7537664 | tf_op jit(solution)/shard_map/dot_general | solution.py:45
  475.2 81.8 %all-reduce.4.cloned.1.call-done = f32[1024,384]{1,0:T(8,128)} async-done(((f32[1024,384]{1,0:T(8,128)}), f32[1024,384]{1,0:T(8,128)}) %all-reduce.4.cloned.1.call-update) | async-done | bytes 1572880 | tf_op jit(solution)/shard_map/psum | solution.py:50
  557.0 0.9 constant_dynamic-slice_fusion
  557.9 0.8 broadcast_in_dim.2
  (23 shorter events, 0.1 us)
Async XLA Ops:
  6.5 2.6 copy-start
  6.5 297.8 %all-reduce.6.cloned.1.call-start = ((), (), s32[]{:S(2)}) async-start(), calls=%async_computation.3 | async-start | bytes 12582912 | tf_op jit(solution)/shard_map/psum | solution.py:34
  9.2 3.0 copy-start.9
  12.2 2.6 copy-start.3
  12.2 2.6 copy-start.2
  13.5 4.4 copy-start.5
  21.0 283.3 %copy-start.1 = (bf16[2048,384]{1,0:T(8,128)(2,1)S(1)}, bf16[2048,384]{1,0:T(8,128)(2,1)}, u32[]{:S(2)}) copy-start(bf16[2048,384]{1,0:T(8,128)(2,1)} %param.9) | copy-start | bytes 4718596
  21.0 283.3 %copy-start.7 = (bf16[2,64,2048]{2,1,0:T(8,128)(2,1)S(1)}, bf16[2,64,2048]{2,1,0:T(8,128)(2,1)}, u32[]{:S(2)}) copy-start(bf16[2,64,2048]{2,1,0:T(8,128)(2,1)} %param.12) | copy-start | bytes 1572868
  21.0 368.1 %all-gather.5.cloned.1.call-start = ((), (), s32[]{:S(2)}) async-start(), calls=%async_computation.1 | async-start | bytes 1622016 | tf_op jit(solution)/shard_map/all_gather | solution.py:38
  307.4 159.6 %all-gather.3.cloned.1.call-start = ((), (), s32[]{:S(2)}) async-start(), calls=%async_computation | async-start | bytes 1622016 | tf_op jit(solution)/shard_map/all_gather | solution.py:38
  307.4 3.1 copy-start.8
  310.5 246.6 %all-reduce.4.cloned.1.call-start = ((), (), s32[]{:S(2)}) async-start(), calls=%async_computation.2 | async-start | bytes 3145728 | tf_op jit(solution)/shard_map/psum | solution.py:50
  395.5 73.6 %copy-start.4 = (bf16[1024,384]{1,0:T(8,128)(2,1)S(1)}, bf16[1024,384]{1,0:T(8,128)(2,1)}, u32[]{:S(2)}) copy-start(bf16[1024,384]{1,0:T(8,128)(2,1)} %copy-done.3) | copy-start | bytes 2359300
  395.5 73.6 %copy-start.6 = (bf16[1024,384]{1,0:T(8,128)(2,1)S(1)}, bf16[1024,384]{1,0:T(8,128)(2,1)}, u32[]{:S(2)}) copy-start(bf16[1024,384]{1,0:T(8,128)(2,1)} %copy-done.5) | copy-start | bytes 2359300
Sparse Core Ops, SparseCore 0:
  21.1 283.1 all-reduce.5
  307.5 81.5 all-gather.4
  391.9 75.0 all-gather.2
  475.3 81.6 all-reduce.3
where the time goes:
time: 566 us; the launch traced here: 565 us
  waiting for transfers between devices  515 us (91%)
  matrix products  31 us (5%)
  between operations  15.2 us (3%)
    psum x1, waiting for transfers between devices, on_device(): lax.psum(jnp.dot(selector, coupled, preferred_element_type=jnp.float32),...  283 us
    all_gather x2, waiting for transfers between devices, on_device(): piece = lax.all_gather(interface_sol, 'sub', axis=0, tiled=True)  149 us
    psum x1, waiting for transfers between devices, on_device(): whole_sum = lax.psum(accumulated, 'shift')  81.8 us
  transfers between devices with their start and end apart: 4, of which 4 were waited for; matrix products, arithmetic and copies ran while one was open for 2% of the time, Pallas kernels for 0%

commit v1 on v0

--- a/solution.py
+++ b/solution.py
@@ -35,7 +35,9 @@
         reduced_all = (interface_rhs.astype(jnp.float32) - summed_all).astype(jnp.bfloat16)
         solved = jnp.dot(schur_local, reduced_all, preferred_element_type=jnp.float32)
         interface_sol = solved.astype(jnp.bfloat16)
-        piece = lax.all_gather(interface_sol, "sub", axis=0, tiled=True)
+        piece = jnp.concatenate(
+            lax.all_to_all(jnp.stack([interface_sol] * lax.axis_size("sub")), "sub", 0, 0), axis=0
+        )
         sources = lax.iota(jnp.int32, piece.shape[0])
         pick_selector = (idx[:, None] == sources[None, :]).astype(jnp.bfloat16)
         picked = jnp.dot(pick_selector, piece, preferred_element_type=jnp.float32)

time: 566 us -> 505 us (0.89)
  waiting for transfers between devices: 515 us -> 437 us
  starting transfers between devices: 0.13 us -> 16.4 us
    all_gather x2 -> x0, waiting for transfers between devices: 149 us -> none  [on_device(): piece = lax.all_gather(interface_sol, 'sub', axis=0, tiled=True)]
    all_to_all x0 -> x2, waiting for transfers between devices: none -> 73.8 us  [on_device(): lax.all_to_all(jnp.stack([interface_sol] * lax.axis_size('sub')), 'sub',...]
    all_to_all x0 -> x2, starting transfers between devices: none -> 16.3 us  [on_device(): lax.all_to_all(jnp.stack([interface_sol] * lax.axis_size('sub')), 'sub',...]
where the time goes in v1:
time: 505 us; the launch traced here: 504 us
  waiting for transfers between devices  437 us (87%)
  matrix products  28.5 us (6%)
  starting transfers between devices  16.4 us (3%)
  between operations  15.5 us (3%)
  local copies, waits for them, and re-layouts  7.22 us (1%)
    psum x1, waiting for transfers between devices, on_device(): lax.psum(jnp.dot(selector, coupled, preferred_element_type=jnp.float32),...  283 us
    psum x1, waiting for transfers between devices, on_device(): whole_sum = lax.psum(accumulated, 'shift')  79.4 us
    all_to_all x2, waiting for transfers between devices, on_device(): lax.all_to_all(jnp.stack([interface_sol] * lax.axis_size('sub')), 'sub',...  73.8 us
    all_to_all x2, starting transfers between devices, on_device(): lax.all_to_all(jnp.stack([interface_sol] * lax.axis_size('sub')), 'sub',...  16.3 us
    dot_general x2, matrix products, on_device(): jnp.dot(inverse, correction, preferred_element_type=jnp.float32)  10.7 us
  transfers between devices with their start and end apart: 4, of which 4 were waited for; matrix products, arithmetic and copies ran while one was open for 2% of the time, Pallas kernels for 0%

profile of v1, /device:TPU:32, one launch (start us, length us, event | category | flops | bytes accessed | tf_op | source)
XLA Modules:
  0.0 504.2 jit_solution(2190951365067894674)
XLA Ops:
  6.5 1.3 dynamic_slice.11
  9.2 3.0 fusion.27
  12.2 1.3 fusion.30
  14.1 0.7 constant_dynamic-slice_fusion.1
  14.8 3.0 fusion.11
  17.9 3.1 fusion.10
  21.0 283.3 %all-reduce.6.cloned.1.call-done = (f32[2048,384]{1,0:T(8,128)}, f32[2048,384]{1,0:T(8,128)}) async-done(((f32[2048,384]{1,0:T(8,128)}, f32[2048,384]{1,0:T(8,128)}), (f32[2048,384]{1,0:T(8,128)}, f32[2048,384]{1,0:T(8,128)})) %all-reduce.6.cloned.1.call-update) | async-done | bytes 6291472 | tf_op jit(solution)/shard_map/psum | solution.py:34
  304.3 2.3 fusion.41
  306.6 1.4 stack.5
  308.0 12.6 %all-to-all-start.1 = ((bf16[32,64,384]{2,1,0:T(8,128)(2,1)}), bf16[32,64,384]{2,1,0:T(8,128)(2,1)}, u32[]{:S(2)}, u32[]{:S(2)}) async-start(bf16[32,64,384]{2,1,0:T(8,128)(2,1)} %stack.5), calls=%async_computation.1 | async-start | bytes 3145728 | tf_op jit(solution)/shard_map/all_to_all | solution.py:39
  320.6 2.3 fusion.44
  322.9 39.4 %all-to-all-done.1 = bf16[32,64,384]{2,1,0:T(8,128)(2,1)} async-done(((bf16[32,64,384]{2,1,0:T(8,128)(2,1)}), bf16[32,64,384]{2,1,0:T(8,128)(2,1)}, u32[]{:S(2)}, u32[]{:S(2)}) %all-to-all-start.1) | async-done | bytes 1572896 | tf_op jit(solution)/shard_map/all_to_all | solution.py:39
  362.4 1.4 stack.4
  363.8 3.8 all-to-all-start
  367.5 0.0 all-reduce.4.cloned.1.call-start
  367.6 0.6 fusion.65
  368.2 2.2 fusion.34
  370.4 4.2 fusion.2
  374.6 34.4 %all-to-all-done = bf16[32,64,384]{2,1,0:T(8,128)(2,1)S(1)} async-done(((bf16[32,64,384]{2,1,0:T(8,128)(2,1)}), bf16[32,64,384]{2,1,0:T(8,128)(2,1)S(1)}, u32[]{:S(2)}, u32[]{:S(2)}) %all-to-all-start) | async-done | bytes 1572896 | tf_op jit(solution)/shard_map/all_to_all | solution.py:39
  408.9 0.8 fusion.33
  409.7 6.4 %fusion.23 = f32[1024,384]{1,0:T(8,128)} fusion(f32[384,1024]{0,1:T(8,128)} %fusion.2, bf16[1024,384]{1,0:T(8,128)(2,1)} %copy-done.4, bf16[1024,384]{1,0:T(8,128)(2,1)} %copy-done.3, bf16[2,1,1024,1024]{3,2,1,0:T(8,128)(2,1)} %param.10, bf16[256,384]{1,0:T(8,128)(2,1)S(1)} %fusion.33, f32[]{:T(128)} %bitcast.10, f32[]{:T(128)} %bitcast, ...), kind=kOutput, calls=%fused_computation.26 | convolution fusion | flops 1009778688 | bytes 7537664 | tf_op jit(solution)/shard_map/dot_general | solution.py:47
  416.2 79.4 %all-reduce.4.cloned.1.call-done = f32[1024,384]{1,0:T(8,128)} async-done(((f32[1024,384]{1,0:T(8,128)}), f32[1024,384]{1,0:T(8,128)}) %all-reduce.4.cloned.1.call-update) | async-done | bytes 1572880 | tf_op jit(solution)/shard_map/psum | solution.py:52
  495.6 0.9 constant_dynamic-slice_fusion
  496.5 0.8 broadcast_in_dim.2
  (19 shorter events, 0.1 us)
Async XLA Ops:
  6.5 2.6 copy-start
  6.5 297.7 %all-reduce.6.cloned.1.call-start = ((), (), s32[]{:S(2)}) async-start(), calls=%async_computation.3 | async-start | bytes 12582912 | tf_op jit(solution)/shard_map/psum | solution.py:34
  9.2 3.0 copy-start.7
  12.2 2.6 copy-start.3
  12.2 2.6 copy-start.2
  13.5 4.4 copy-start.4
  21.0 283.3 %copy-start.1 = (bf16[2048,384]{1,0:T(8,128)(2,1)S(1)}, bf16[2048,384]{1,0:T(8,128)(2,1)}, u32[]{:S(2)}) copy-start(bf16[2048,384]{1,0:T(8,128)(2,1)} %param.9) | copy-start | bytes 4718596
  21.0 283.3 %copy-start.5 = (bf16[2,64,2048]{2,1,0:T(8,128)(2,1)S(1)}, bf16[2,64,2048]{2,1,0:T(8,128)(2,1)}, u32[]{:S(2)}) copy-start(bf16[2,64,2048]{2,1,0:T(8,128)(2,1)} %param.12) | copy-start | bytes 1572868
  308.0 54.4 %all-to-all-start.1 = ((bf16[32,64,384]{2,1,0:T(8,128)(2,1)}), bf16[32,64,384]{2,1,0:T(8,128)(2,1)}, u32[]{:S(2)}, u32[]{:S(2)}) async-start(bf16[32,64,384]{2,1,0:T(8,128)(2,1)} %stack.5), calls=%async_computation.1 | async-start | bytes 3145728 | tf_op jit(solution)/shard_map/all_to_all | solution.py:39
  322.9 44.7 %copy-start.6 = (f32[2]{0:T(128)S(1)}, f32[2]{0:T(128)}, u32[]{:S(2)}) copy-start(f32[2]{0:T(128)} %param.13) | copy-start | bytes 28
  363.8 45.2 %all-to-all-start = ((bf16[32,64,384]{2,1,0:T(8,128)(2,1)}), bf16[32,64,384]{2,1,0:T(8,128)(2,1)S(1)}, u32[]{:S(2)}, u32[]{:S(2)}) async-start(bf16[32,64,384]{2,1,0:T(8,128)(2,1)} %stack.4), calls=%async_computation | async-start | bytes 3145728 | tf_op jit(solution)/shard_map/all_to_all | solution.py:39
  367.5 128.0 %all-reduce.4.cloned.1.call-start = ((), (), s32[]{:S(2)}) async-start(), calls=%async_computation.2 | async-start | bytes 3145728 | tf_op jit(solution)/shard_map/psum | solution.py:52
Sparse Core Ops, SparseCore 0:
  21.1 283.1 all-reduce.5
  416.3 79.2 all-reduce.3
